TPU v7x, 512 devices: a whole 4x4x16 slice. The times are simulated.
512 devices in a mesh: bis: 128 (over z, y, x_lo), src: 4 (over x_hi, core).
Axes of the slice: x: 4 (x_hi: 2, x_lo: 2; x = x_hi * 2 + x_lo), y: 4, z: 16, core: 2. Of those that a mesh axis runs over, the one named last changes fastest.
Arguments:
- coefficients: float32 [4, 2, 64, 32768], P('src', None, None, 'bis'), may hold values from -6 to 6
- factors: float32 [4, 3, 2048, 64, 256], P('src', None, 'bis'), may hold values from -0.375 to 0.375
Outputs:
- potentials: float32 [2, 64, 32768], P(None, 'src', 'bis')
All inputs are finite; a program needn't handle non-finite values.
Results may differ from a plain program's by a relative error of at most 0.0001.
Values sent between devices are 32-bit elements; how exact they have to be, the bound alone decides.
A program may use at most 64 MiB of HBM per device.

v0:
```python
import jax
import jax.numpy as jnp
from jax import lax
from jax.sharding import PartitionSpec as P

LEVELS = 3


def swapped(value, axis, stride):
    mask = 2**stride
    pairs = [(source, source ^ mask) for source in range(lax.axis_size(axis))]
    return lax.ppermute(value, axis, pairs)


def mix_blocks(factor, stacked):
    return jnp.einsum("boj,jbk->obk", factor, stacked, precision=lax.Precision.HIGHEST)


def advance(state, factor, bit):
    real_part = state[0]
    imag_part = state[1]
    partner = swapped(state, "bis", bit)
    other_re = partner[0]
    other_im = partner[1]
    stack_re = jnp.concatenate([real_part, -imag_part, other_re, -other_im], axis=0)
    stack_im = jnp.concatenate([imag_part, real_part, other_im, other_re], axis=0)
    new_re = mix_blocks(factor, stack_re)
    new_im = mix_blocks(factor, stack_im)
    return jnp.stack([new_re, new_im], axis=0)


def per_device(coefficients, factors):
    middle = (lax.axis_size("bis").bit_length() - 1) // 2
    rank = coefficients.shape[2]
    columns = coefficients.shape[3]
    blocks = factors.shape[2]
    state = coefficients[0].reshape(2, rank, blocks, columns // blocks)
    for level_num in range(LEVELS):
        state = advance(state, factors[0, level_num], middle + 1 - level_num)
    flat = state.reshape(2, rank, columns)
    total = lax.psum(flat, "src")
    share = rank // lax.axis_size("src")
    start = lax.axis_index("src") * share
    return lax.dynamic_slice_in_dim(total, start, share, 1)


def solution(mesh):
    placed = (P("src", None, None, "bis"), P("src", None, "bis", None, None))
    return jax.shard_map(
        per_device, mesh=mesh, in_specs=placed, out_specs=P(None, "src", "bis"), check_vma=False
    )
```

profile of v0, /device:TPU:1, one launch (start us, length us, event | category | flops | bytes accessed | tf_op | source)
XLA Modules:
  0.0 131.5 jit_solution(13678017385581789084)
XLA Ops:
  6.5 0.0 copy-start
  6.5 0.0 all-reduce.2.cloned.1.call-start
  6.5 1.9 %copy.5 = f32[1,2,64,256]{2,3,1,0:T(8,128)} copy(f32[1,2,64,256]{3,2,1,0:T(8,128)} %param.2) | data formatting | bytes 262144 | tf_op args[0]
  8.4 5.7 %collective-permute-start = (f32[2,64,16,16]{1,3,2,0:T(8,128)}, f32[2,64,16,16]{1,3,2,0:T(8,128)}, u32[]{:S(2)}, u32[]{:S(2)}) collective-permute-start(f32[2,64,16,16]{1,3,2,0:T(8,128)} %bitcast.2), channel_id=1, source_target_pairs={{0,64},{4,68},{8,72},{12,76},{16,80},{20,84},{24,88},{28,92},{32,9... | collective-permute-start | bytes 393224 | tf_op jit(solution)/shard_map/ppermute | solution.py:12
  14.2 1.5 %fusion.69 = (f32[1,1,64,256]{3,2,1,0:T(8,128)S(1)}, f32[1,1,64,256]{3,2,1,0:T(8,128)}) fusion(f32[1,2,64,256]{3,2,1,0:T(8,128)} %param.2), kind=kLoop, calls=%fused_computation.81 | loop fusion | bytes 262144 | tf_op jit(solution)/shard_map/slice | solution.py:21
  15.7 0.1 copy.4
  15.8 0.9 copy.3
  16.7 8.7 %collective-permute-done = f32[2,64,16,16]{1,3,2,0:T(8,128)} collective-permute-done((f32[2,64,16,16]{1,3,2,0:T(8,128)}, f32[2,64,16,16]{1,3,2,0:T(8,128)}, u32[]{:S(2)}, u32[]{:S(2)}) %collective-permute-start) | collective-permute-done | bytes 131104 | tf_op jit(solution)/shard_map/ppermute | solution.py:12
  25.4 1.0 slice_bitcast_fusion.4
  26.4 2.3 %bitcast_negate_fusion.1 = (f32[64,16,16]{0,2,1:T(8,128)S(1)}, f32[16,16,64]{2,1,0:T(8,128)S(1)}) fusion(f32[1,3,16,64,256]{4,3,2,1,0:T(8,128)} %param.3, f32[64,16,16]{0,2,1:T(8,128)S(1)} %get-tuple-element.10, f32[64,16,16]{0,2,1:T(8,128)S(1)} %get-tuple-element.9, f32[64,16,16]{0,2,1:T(8,128)S(1)} %bitcast.70, f32[64,16,16]{0,2,1:T(8,128)S(1)} %bitcast.69), kind=kOutput, calls=%fused_computation.77 | convolution fusion | flops 50544640 | bytes 1441792 | tf_op jit(solution)/shard_map/boj,jbk->obk/dot_general | solution.py:16
  28.7 0.9 fusion.66
  29.6 0.0 copy-done
  29.6 1.1 fusion.10
  30.7 3.8 %collective-permute-start.1 = (f32[2,64,16,16]{1,3,2,0:T(8,128)S(1)}, f32[2,64,16,16]{1,3,2,0:T(8,128)S(1)}, u32[]{:S(2)}, u32[]{:S(2)}) collective-permute-start(f32[2,64,16,16]{1,3,2,0:T(8,128)S(1)} %pad_maximum_fusion), channel_id=1, source_target_pairs={{0,32},{4,36},{8,40},{12,44},{16,48},{20,52},{24,56},{28,60},{32,0... | collective-permute-start | bytes 393224 | tf_op jit(solution)/shard_map/ppermute | solution.py:12
  34.5 5.2 %collective-permute-done.1 = f32[2,64,16,16]{1,3,2,0:T(8,128)S(1)} collective-permute-done((f32[2,64,16,16]{1,3,2,0:T(8,128)S(1)}, f32[2,64,16,16]{1,3,2,0:T(8,128)S(1)}, u32[]{:S(2)}, u32[]{:S(2)}) %collective-permute-start.1) | collective-permute-done | bytes 131104 | tf_op jit(solution)/shard_map/ppermute | solution.py:12
  39.7 1.1 fusion.6
  40.7 1.1 bitcast_negate_fusion
  41.8 5.0 %collective-permute-start.2 = (f32[2,64,16,16]{1,3,2,0:T(8,128)S(1)}, f32[2,64,16,16]{1,3,2,0:T(8,128)S(1)}, u32[]{:S(2)}, u32[]{:S(2)}) collective-permute-start(f32[2,64,16,16]{1,3,2,0:T(8,128)S(1)} %pad_maximum_fusion.1), channel_id=1, source_target_pairs={{0,16},{4,20},{8,24},{12,28},{16,0},{20,4},{24,8},{28,12},{32,48},... | collective-permute-start | bytes 393224 | tf_op jit(solution)/shard_map/ppermute | solution.py:12
  46.9 4.4 %collective-permute-done.2 = f32[2,64,16,16]{1,3,2,0:T(8,128)S(1)} collective-permute-done((f32[2,64,16,16]{1,3,2,0:T(8,128)S(1)}, f32[2,64,16,16]{1,3,2,0:T(8,128)S(1)}, u32[]{:S(2)}, u32[]{:S(2)}) %collective-permute-start.2) | collective-permute-done | bytes 131104 | tf_op jit(solution)/shard_map/ppermute | solution.py:12
  51.3 0.0 copy-start.1
  51.3 0.7 copy-done.1
  52.0 1.7 %fusion = f32[16,16,64]{2,1,0:T(8,128)} fusion(f32[1,3,16,64,256]{4,3,2,1,0:T(8,128)S(1)} %copy-done, f32[64,16,16]{0,2,1:T(8,128)S(1)} %get-tuple-element.6, f32[64,16,16]{0,2,1:T(8,128)S(1)} %get-tuple-element.5, f32[64,16,16]{0,2,1:T(8,128)S(1)} %bitcast.64, f32[64,16,16]{0,2,1:T(8,128)S(1)} %bitcast.73), kind=kOutput, calls=%fused_computation | convolution fusion | flops 50528256 | bytes 1638400 | tf_op jit(solution)/shard_map/boj,jbk->obk/dot_general | solution.py:16
  53.7 1.6 %copy.7 = f32[1,64,256]{2,1,0:T(8,128)} copy(f32[1,64,256]{1,2,0:T(8,128)} %bitcast.75) | data formatting | bytes 131072 | tf_op jit(solution)/shard_map/stack | solution.py:29
  55.3 0.9 fusion.68
  56.3 1.7 %fusion.2 = f32[16,16,64]{2,1,0:T(8,128)} fusion(f32[1,3,16,64,256]{4,3,2,1,0:T(8,128)S(1)} %copy-done, f32[64,16,16]{0,2,1:T(8,128)S(1)} %fusion.68, f32[64,16,16]{0,2,1:T(8,128)S(1)} %get-tuple-element.6, f32[64,16,16]{0,2,1:T(8,128)S(1)} %get-tuple-element.15, f32[64,16,16]{0,2,1:T(8,128)S(1)} %bitcast.65), kind=kOutput, calls=%fused_computation.2 | convolution fusion | flops 50528256 | bytes 1638400 | tf_op jit(solution)/shard_map/boj,jbk->obk/dot_general | solution.py:16
  58.0 1.0 copy.6
  59.0 1.5 %pad_maximum_fusion.2 = f32[2,64,256]{2,1,0:T(8,128)} fusion(f32[1,64,256]{2,1,0:T(8,128)} %copy.7, f32[1,64,256]{2,1,0:T(8,128)S(1)} %copy.6), kind=kLoop, calls=%fused_computation.68 | loop fusion | flops 32768 | bytes 262144 | tf_op jit(solution)/shard_map/stack | solution.py:29
  60.4 0.0 all-reduce.2.cloned.1.call-update
  60.5 62.8 %all-reduce.2.cloned.1.call-done = f32[2,64,256]{2,1,0:T(8,128)} async-done(((f32[2,64,256]{2,1,0:T(8,128)}), f32[2,64,256]{2,1,0:T(8,128)}) %all-reduce.2.cloned.1.call-update) | async-done | bytes 131088 | tf_op jit(solution)/shard_map/psum | solution.py:41
  123.3 1.4 %constant_dynamic-slice_fusion = f32[2,16,256]{2,1,0:T(8,128)} fusion(f32[2,64,256]{2,1,0:T(8,128)} %all-reduce.2.cloned.1.call-done, s32[]{:T(128)S(6)} %select_n.3), kind=kLoop, calls=%fused_computation.69 | loop fusion | bytes 65540 | tf_op jit(solution)/shard_map/dynamic_slice | solution.py:44
  (6 shorter events, 0.1 us)
Async XLA Ops:
  6.5 23.1 %copy-start = (f32[1,3,16,64,256]{4,3,2,1,0:T(8,128)S(1)}, f32[1,3,16,64,256]{4,3,2,1,0:T(8,128)}, u32[]{:S(2)}) copy-start(f32[1,3,16,64,256]{4,3,2,1,0:T(8,128)} %param.3) | copy-start | bytes 9437188
  6.5 116.7 %all-reduce.2.cloned.1.call-start = ((), (), s32[]{:S(2)}) async-start(), calls=%async_computation | async-start | bytes 262144 | tf_op jit(solution)/shard_map/psum | solution.py:41
  8.4 17.0 %collective-permute-start = (f32[2,64,16,16]{1,3,2,0:T(8,128)}, f32[2,64,16,16]{1,3,2,0:T(8,128)}, u32[]{:S(2)}, u32[]{:S(2)}) collective-permute-start(f32[2,64,16,16]{1,3,2,0:T(8,128)} %bitcast.2), channel_id=1, source_target_pairs={{0,64},{4,68},{8,72},{12,76},{16,80},{20,84},{24,88},{28,92},{32,9... | collective-permute-start | bytes 393224 | tf_op jit(solution)/shard_map/ppermute | solution.py:12
  30.7 8.9 %collective-permute-start.1 = (f32[2,64,16,16]{1,3,2,0:T(8,128)S(1)}, f32[2,64,16,16]{1,3,2,0:T(8,128)S(1)}, u32[]{:S(2)}, u32[]{:S(2)}) collective-permute-start(f32[2,64,16,16]{1,3,2,0:T(8,128)S(1)} %pad_maximum_fusion), channel_id=1, source_target_pairs={{0,32},{4,36},{8,40},{12,44},{16,48},{20,52},{24,56},{28,60},{32,0... | collective-permute-start | bytes 393224 | tf_op jit(solution)/shard_map/ppermute | solution.py:12
  41.8 9.5 %collective-permute-start.2 = (f32[2,64,16,16]{1,3,2,0:T(8,128)S(1)}, f32[2,64,16,16]{1,3,2,0:T(8,128)S(1)}, u32[]{:S(2)}, u32[]{:S(2)}) collective-permute-start(f32[2,64,16,16]{1,3,2,0:T(8,128)S(1)} %pad_maximum_fusion.1), channel_id=1, source_target_pairs={{0,16},{4,20},{8,24},{12,28},{16,0},{20,4},{24,8},{28,12},{32,48},... | collective-permute-start | bytes 393224 | tf_op jit(solution)/shard_map/ppermute | solution.py:12
  51.3 0.7 copy-start.1
Sparse Core Ops, SparseCore 0:
  60.6 62.6 all-reduce.1
where the time goes:
time: 132 us; the launch traced here: 131 us
  waiting for transfers between devices  81.1 us (61%)
  starting transfers between devices  14.5 us (11%)
  between operations  13.5 us (10%)
  local copies, waits for them, and re-layouts  10.1 us (8%)
  matrix products  8.87 us (7%)
  other arithmetic  3.4 us (3%)
    psum x1, waiting for transfers between devices, per_device(): total = lax.psum(flat, 'src')  62.8 us
    ppermute x3, waiting for transfers between devices, swapped(): return lax.ppermute(value, axis, pairs)  18.3 us
    ppermute x3, starting transfers between devices, swapped(): return lax.ppermute(value, axis, pairs)  14.5 us
    dot_general x6, matrix products, mix_blocks(): jnp.einsum('boj,jbk->obk', factor, stacked, precision=lax.Precision.HIGHEST)  8.87 us
  transfers between devices with their start and end apart: 4, of which 4 were waited for; matrix products, arithmetic and copies ran while one was open for 2% of the time, Pallas kernels for 0%

commit v1 on v0

v1 whole, which is shorter than its diff:
```python
import functools

import jax
import jax.numpy as jnp
from jax import lax
from jax.experimental import pallas as pl
from jax.experimental.pallas import tpu as pltpu
from jax.sharding import PartitionSpec as P

LEVELS = 3
MESH = pl.DeviceIdType.MESH
LANES = 128


def flipped(index, step):
    return index + step - 2 * step * ((index // step) % 2)


def split(value):
    high = value.astype(jnp.bfloat16)
    low = (value - high.astype(jnp.float32)).astype(jnp.bfloat16)
    return high, low


def stacked(xr, xi, pr, pi):
    real = jnp.concatenate([xr, -xi, pr, -pi], axis=0)
    imag = jnp.concatenate([xi, xr, pi, pr], axis=0)
    return jnp.concatenate([real, imag], axis=1)


def kernel(steps, groups, rank, blocks, per_block,
           coef, fac, out,
           start, fbuf, fhigh, flow, recv, state, shares,
           coef_sem, fac_sem, send_sem, recv_sem, share_send, share_recv):
    halves = coef.shape[3] // LANES
    half_blocks = blocks // halves
    bis = lax.axis_index("bis")
    src = lax.axis_index("src")
    share = rank // groups
    partners = [flipped(bis, step) for step in steps]
    peers = []
    for k in range(1, groups):
        peer = src
        for bit in range(groups.bit_length() - 1):
            if (k >> bit) & 1:
                peer = flipped(peer, 1 << bit)
        peers.append(peer)

    coef_copy = pltpu.make_async_copy(coef.at[0], start, coef_sem)
    coef_copy.start()
    fac_copies = [
        pltpu.make_async_copy(fac.at[0, l], fbuf.at[l], fac_sem.at[l]) for l in range(LEVELS)
    ]
    for copy in fac_copies:
        copy.start()

    barrier = pltpu.get_barrier_semaphore()
    for partner in partners:
        pl.semaphore_signal(barrier, inc=1, device_id={"bis": partner}, device_id_type=MESH)
    for peer in peers:
        pl.semaphore_signal(barrier, inc=1, device_id={"src": peer}, device_id_type=MESH)
    pl.semaphore_wait(barrier, len(partners) + len(peers))

    def exchange(level, half):
        if level == 0:
            source = coef.at[0, :, :, pl.ds(half * LANES, LANES)]
        else:
            source = state.at[level - 1, half]
        return pltpu.make_async_remote_copy(
            src_ref=source,
            dst_ref=recv.at[level, half],
            send_sem=send_sem.at[level, half],
            recv_sem=recv_sem.at[level, half],
            device_id={"bis": partners[level]},
            device_id_type=MESH,
        )

    def share_copy(k, half):
        return pltpu.make_async_remote_copy(
            src_ref=state.at[LEVELS - 1, half, :, pl.ds(peers[k] * share, share), :],
            dst_ref=shares.at[k, half],
            send_sem=share_send.at[k, half],
            recv_sem=share_recv.at[k, half],
            device_id={"src": peers[k]},
            device_id_type=MESH,
        )

    for half in range(halves):
        exchange(0, half).start()
    for level in range(LEVELS):
        fac_copies[level].wait()
        high, low = split(fbuf[level])
        fhigh[level] = high
        flow[level] = low
    coef_copy.wait()

    lane_block = lax.broadcasted_iota(jnp.int32, (rank, 2 * LANES), 1) % LANES // per_block
    for level in range(LEVELS):
        for half in range(halves):
            copy = exchange(level, half)
            copy.wait_recv()
            if level == 0:
                own = start[:, :, half * LANES:(half + 1) * LANES]
            else:
                own = state[level - 1, half]
            other = recv[level, half]
            own_h, own_l = split(own)
            other_h, other_l = split(other)
            wh = stacked(own_h[0], own_h[1], other_h[0], other_h[1])
            wl = stacked(own_l[0], own_l[1], other_l[0], other_l[1])
            fh = fhigh[level, half * half_blocks:(half + 1) * half_blocks].reshape(half_blocks * rank, 4 * rank)
            fl = flow[level, half * half_blocks:(half + 1) * half_blocks].reshape(half_blocks * rank, 4 * rank)
            product = (
                jnp.dot(fh, wh, preferred_element_type=jnp.float32)
                + jnp.dot(fh, wl, preferred_element_type=jnp.float32)
                + jnp.dot(fl, wh, preferred_element_type=jnp.float32)
            )
            picked = product[0:rank]
            for b in range(1, half_blocks):
                picked = jnp.where(lane_block == b, product[b * rank:(b + 1) * rank], picked)
            state[level, half, 0] = picked[:, :LANES]
            state[level, half, 1] = picked[:, LANES:]
            if level + 1 < LEVELS:
                exchange(level + 1, half).start()
            else:
                for k in range(groups - 1):
                    share_copy(k, half).start()
    for half in range(halves):
        total = state[LEVELS - 1, half, :, pl.ds(pl.multiple_of(src * share, share), share), :]
        for k in range(groups - 1):
            share_copy(k, half).wait_recv()
            total = total + shares[k, half]
        out[:, :, half * LANES:(half + 1) * LANES] = total
    for level in range(LEVELS):
        for half in range(halves):
            exchange(level, half).wait_send()
    for half in range(halves):
        for k in range(groups - 1):
            share_copy(k, half).wait_send()


def per_device(coefficients, factors):
    middle = (lax.axis_size("bis").bit_length() - 1) // 2
    groups = lax.axis_size("src")
    _, _, rank, columns = coefficients.shape
    blocks = factors.shape[2]
    halves = columns // LANES
    share = rank // groups
    steps = [2 ** (middle + 1 - l) for l in range(LEVELS)]
    body = functools.partial(kernel, steps, groups, rank, blocks, columns // blocks)
    return pl.pallas_call(
        body,
        out_shape=jax.ShapeDtypeStruct((2, share, columns), jnp.float32),
        in_specs=[pl.BlockSpec(memory_space=pl.ANY)] * 2,
        out_specs=pl.BlockSpec(memory_space=pltpu.VMEM),
        scratch_shapes=[
            pltpu.VMEM((2, rank, columns), jnp.float32),
            pltpu.VMEM((LEVELS, blocks, rank, 4 * rank), jnp.float32),
            pltpu.VMEM((LEVELS, blocks, rank, 4 * rank), jnp.bfloat16),
            pltpu.VMEM((LEVELS, blocks, rank, 4 * rank), jnp.bfloat16),
            pltpu.VMEM((LEVELS, halves, 2, rank, LANES), jnp.float32),
            pltpu.VMEM((LEVELS, halves, 2, rank, LANES), jnp.float32),
            pltpu.VMEM((groups - 1, halves, 2, share, LANES), jnp.float32),
            pltpu.SemaphoreType.DMA,
            pltpu.SemaphoreType.DMA((LEVELS,)),
            pltpu.SemaphoreType.DMA((LEVELS, halves)),
            pltpu.SemaphoreType.DMA((LEVELS, halves)),
            pltpu.SemaphoreType.DMA((groups - 1, halves)),
            pltpu.SemaphoreType.DMA((groups - 1, halves)),
        ],
        compiler_params=pltpu.CompilerParams(
            collective_id=0, has_side_effects=True, vmem_limit_bytes=60 * 1024 * 1024
        ),
    )(coefficients, factors)


def solution(mesh):
    placed = (P("src", None, None, "bis"), P("src", None, "bis", None, None))
    return jax.shard_map(
        per_device, mesh=mesh, in_specs=placed, out_specs=P(None, "src", "bis"), check_vma=False
    )
```

time: 132 us -> 29.9 us (0.23)
  waiting for transfers between devices: 81.1 us -> 0 us
  Pallas kernels: 0 us -> 28.3 us
  starting transfers between devices: 14.5 us -> 0 us
  between operations: 13.5 us -> 0.01 us
  matrix products: 8.87 us -> 0 us
  local copies, waits for them, and re-layouts: 10.1 us -> 1.38 us
  other arithmetic: 3.4 us -> 0 us
    psum x1 -> x0, waiting for transfers between devices: 62.8 us -> none  [per_device(): total = lax.psum(flat, 'src')]
    pallas_call x0 -> x1, Pallas kernels: none -> 28.3 us  [per_device(): pl.pallas_call(body, out_shape=jax.ShapeDtypeStruct((2, share, columns),...]
    ppermute x3 -> x0, waiting for transfers between devices: 18.3 us -> none  [swapped(): return lax.ppermute(value, axis, pairs)]
    ppermute x3 -> x0, starting transfers between devices: 14.5 us -> none  [swapped(): return lax.ppermute(value, axis, pairs)]
    dot_general x6 -> x0, matrix products: 8.87 us -> none  [mix_blocks(): jnp.einsum('boj,jbk->obk', factor, stacked, precision=lax.Precision.HIGHEST)]
    another operation x2 -> x0, local copies, waits for them, and re-layouts: 2.58 us -> none  [advance(): return jnp.stack([new_re, new_im], axis=0)]
    slice x3 -> x0, local copies, waits for them, and re-layouts: 2.52 us -> none  [the longest x2 1.59 us: advance(): imag_part = state[1]]
    neg x4 -> x0, other arithmetic: 1.86 us -> none  [the longest x3 1.85 us: advance(): -other_im]
  transfers between devices with their start and end apart: 4 -> 0, of which waited for: 4 -> 0; matrix products, arithmetic and copies ran while one was open for 2% -> 0% of each run, Pallas kernels for 0% -> 0%
where the time goes in v1:
time: 29.9 us; the launch traced here: 29.7 us
  Pallas kernels  28.3 us (95%)
  local copies, waits for them, and re-layouts  1.38 us (5%)
    pallas_call x1, Pallas kernels, per_device(): pl.pallas_call(body, out_shape=jax.ShapeDtypeStruct((2, share, columns),...  28.3 us
    unnamed x1, local copies, waits for them, and re-layouts  1.38 us

profile of v1, /device:TPU:1, one launch (start us, length us, event | category | flops | bytes accessed | tf_op | source)
XLA Modules:
  0.0 29.7 jit_solution(18298097819470242767)
XLA Ops:
  0.0 28.3 %shard_map.28 = f32[2,16,256]{2,1,0:T(8,128)} custom-call(f32[1,2,64,256]{3,2,1,0:T(8,128)} %coef.1, f32[1,3,16,64,256]{4,3,2,1,0:T(8,128)} %fac.1), custom_call_target="tpu_custom_call" | custom-call | tf_op jit(solution)/shard_map/pallas_call | solution.py:151
  28.3 1.4 %copy.4 = f32[2,16,256]{2,1,0:T(8,128)} copy(f32[2,16,256]{2,1,0:T(8,128)} %shard_map.28) | data formatting | bytes 65536

commit v2 on v0

v2 whole, which is shorter than its diff:
```python
import functools

import jax
import jax.numpy as jnp
from jax import lax
from jax.experimental import pallas as pl
from jax.experimental.pallas import tpu as pltpu
from jax.sharding import PartitionSpec as P

LEVELS = 3
MESH = pl.DeviceIdType.MESH
LANES = 128
HALF = LANES // 2


def flipped(index, step):
    return index + step - 2 * step * ((index // step) % 2)


def turned(packed, low_half):
    moved = pltpu.roll(packed, HALF, 1)
    return jnp.where(low_half, -moved, moved)


def kernel(steps, groups, rank, blocks, per_block,
           coef, fac, out,
           start, fbuf, fsplit, first, recv, state, shares,
           coef_sem, fac_sem, first_sem, send_sem, recv_sem, share_send, share_recv, ready):
    chunks = blocks * per_block // HALF
    chunk_blocks = blocks // chunks
    rows = chunk_blocks * rank
    bis = lax.axis_index("bis")
    src = lax.axis_index("src")
    share = rank // groups
    partners = [flipped(bis, step) for step in steps]
    peers = []
    for k in range(1, groups):
        peer = src
        for bit in range(groups.bit_length() - 1):
            if (k >> bit) & 1:
                peer = flipped(peer, 1 << bit)
        peers.append(peer)

    coef_copy = pltpu.make_async_copy(coef.at[0], start, coef_sem)
    coef_copy.start()
    fac_copies = [
        pltpu.make_async_copy(fac.at[0, l], fbuf.at[l], fac_sem.at[l]) for l in range(LEVELS)
    ]
    for copy in fac_copies:
        copy.start()

    waits = [bis // steps[1] % 2, bis // steps[2] % 2]
    links = [{"bis": partners[1]}, {"bis": partners[2]}]
    for k in range(1, groups):
        waits.append(src // 2 % 2 if k >= 2 else 1 - src % 2)
        links.append({"src": peers[k - 1]})
    barrier = pltpu.get_barrier_semaphore()
    pl.semaphore_signal(barrier, inc=1, device_id={"bis": partners[0]}, device_id_type=MESH)
    for late, link in zip(waits, links):
        @pl.when(late == 0)
        def _(link=link):
            pl.semaphore_signal(barrier, inc=1, device_id=link, device_id_type=MESH)
    pl.semaphore_wait(barrier, 1 + sum(waits))

    def answered(i):
        @pl.when(waits[i] == 0)
        def _():
            pl.semaphore_wait(ready.at[i], 1)

    first_copy = pltpu.make_async_remote_copy(
        src_ref=coef.at[0, :, :, pl.ds(0, LANES)],
        dst_ref=first,
        send_sem=first_sem.at[0],
        recv_sem=first_sem.at[1],
        device_id={"bis": partners[0]},
        device_id_type=MESH,
    )
    first_copy.start()

    for i, (late, link) in enumerate(zip(waits, links)):
        @pl.when(late == 1)
        def _(i=i, link=link):
            pl.semaphore_signal(ready.at[i], inc=1, device_id=link, device_id_type=MESH)

    def exchange(level, chunk):
        return pltpu.make_async_remote_copy(
            src_ref=state.at[level, chunk],
            dst_ref=recv.at[level, chunk],
            send_sem=send_sem.at[level, chunk],
            recv_sem=recv_sem.at[level, chunk],
            device_id={"bis": partners[level]},
            device_id_type=MESH,
        )

    def share_copy(k, chunk):
        return pltpu.make_async_remote_copy(
            src_ref=state.at[LEVELS, chunk, pl.ds(pl.multiple_of(peers[k] * share, share), share), :],
            dst_ref=shares.at[k, chunk],
            send_sem=share_send.at[k, chunk],
            recv_sem=share_recv.at[k, chunk],
            device_id={"src": peers[k]},
            device_id_type=MESH,
        )

    low_half = lax.broadcasted_iota(jnp.int32, (rank, LANES), 1) < HALF
    lane_block = lax.broadcasted_iota(jnp.int32, (rank, LANES), 1) % HALF // per_block

    def packed(pair, chunk):
        real, imag = pair
        if chunk % 2 == 0:
            imag = pltpu.roll(imag, HALF, 1)
        else:
            real = pltpu.roll(real, HALF, 1)
        return jnp.where(low_half, real, imag)

    coef_copy.wait()
    for chunk in list(range(2, chunks)) + [0, 1]:
        tile = chunk // 2 * LANES
        state[0, chunk] = packed((start[0, :, tile:tile + LANES], start[1, :, tile:tile + LANES]), chunk)
        if chunk >= 2:
            exchange(0, chunk).start()

    for level in range(LEVELS):
        fac_copies[level].wait()

        def split_block(block, carry, level=level):
            value = fbuf[level, block]
            high = value.astype(jnp.bfloat16)
            low = (value - high.astype(jnp.float32)).astype(jnp.bfloat16)
            chunk = block // chunk_blocks
            row = pl.multiple_of(block % chunk_blocks * rank, rank)
            fsplit[level, chunk, pl.ds(row, rank), :] = high
            fsplit[level, chunk, pl.ds(row + rows, rank), :] = low
            return carry

        lax.fori_loop(0, blocks, split_block, 0)

    def step(level, chunk):
        own = state[level, chunk]
        if level == 0 and chunk < 2:
            if chunk == 0:
                first_copy.wait_recv()
            other = packed((first[0], first[1]), chunk)
        else:
            exchange(level, chunk).wait_recv()
            other = recv[level, chunk]
        weights = jnp.concatenate([own, turned(own, low_half), other, turned(other, low_half)], axis=0)
        high = weights.astype(jnp.bfloat16)
        low = (weights - high.astype(jnp.float32)).astype(jnp.bfloat16)
        fh = fsplit[level, chunk, :rows]
        fl = fsplit[level, chunk, rows:]
        product = jnp.dot(fh, jnp.concatenate([high, low], axis=1), preferred_element_type=jnp.float32)
        summed = product[:, :LANES] + product[:, LANES:] + jnp.dot(fl, high, preferred_element_type=jnp.float32)
        picked = summed[0:rank]
        for b in range(1, chunk_blocks):
            picked = jnp.where(lane_block == b, summed[b * rank:(b + 1) * rank], picked)
        state[level + 1, chunk] = picked
        if level + 1 < LEVELS:
            if chunk == 0:
                answered(level)
            exchange(level + 1, chunk).start()
        else:
            for k in range(groups - 1):
                if chunk == 0:
                    answered(LEVELS - 1 + k)
                share_copy(k, chunk).start()

    for level in range(LEVELS):
        for chunk in range(chunks):
            step(level, chunk)

    own_rows = pl.ds(pl.multiple_of(src * share, share), share)
    low_share = lax.broadcasted_iota(jnp.int32, (share, LANES), 1) < HALF
    for pair in range(chunks // 2):
        totals = []
        for chunk in (2 * pair, 2 * pair + 1):
            total = state[LEVELS, chunk, own_rows, :]
            for k in range(groups - 1):
                share_copy(k, chunk).wait_recv()
                total = total + shares[k, chunk]
            totals.append(total)
        tile = pair * LANES
        out[0, :, tile:tile + LANES] = jnp.where(low_share, totals[0], pltpu.roll(totals[1], HALF, 1))
        out[1, :, tile:tile + LANES] = jnp.where(low_share, pltpu.roll(totals[0], HALF, 1), totals[1])
    first_copy.wait_send()
    for level in range(LEVELS):
        for chunk in range(chunks):
            if level > 0 or chunk >= 2:
                exchange(level, chunk).wait_send()
    for chunk in range(chunks):
        for k in range(groups - 1):
            share_copy(k, chunk).wait_send()


def per_device(coefficients, factors):
    middle = (lax.axis_size("bis").bit_length() - 1) // 2
    groups = lax.axis_size("src")
    _, _, rank, columns = coefficients.shape
    blocks = factors.shape[2]
    chunks = columns // HALF
    share = rank // groups
    steps = [2 ** (middle + 1 - l) for l in range(LEVELS)]
    body = functools.partial(kernel, steps, groups, rank, blocks, columns // blocks)
    return pl.pallas_call(
        body,
        out_shape=jax.ShapeDtypeStruct((2, share, columns), jnp.float32),
        in_specs=[pl.BlockSpec(memory_space=pl.ANY)] * 2,
        out_specs=pl.BlockSpec(memory_space=pltpu.VMEM),
        scratch_shapes=[
            pltpu.VMEM((2, rank, columns), jnp.float32),
            pltpu.VMEM((LEVELS, blocks, rank, 4 * rank), jnp.float32),
            pltpu.VMEM((LEVELS, chunks, 2 * blocks // chunks * rank, 4 * rank), jnp.bfloat16),
            pltpu.VMEM((2, rank, LANES), jnp.float32),
            pltpu.VMEM((LEVELS, chunks, rank, LANES), jnp.float32),
            pltpu.VMEM((LEVELS + 1, chunks, rank, LANES), jnp.float32),
            pltpu.VMEM((groups - 1, chunks, share, LANES), jnp.float32),
            pltpu.SemaphoreType.DMA,
            pltpu.SemaphoreType.DMA((LEVELS,)),
            pltpu.SemaphoreType.DMA((2,)),
            pltpu.SemaphoreType.DMA((LEVELS, chunks)),
            pltpu.SemaphoreType.DMA((LEVELS, chunks)),
            pltpu.SemaphoreType.DMA((groups - 1, chunks)),
            pltpu.SemaphoreType.DMA((groups - 1, chunks)),
            pltpu.SemaphoreType.REGULAR((LEVELS + groups - 2,)),
        ],
        compiler_params=pltpu.CompilerParams(
            collective_id=0, has_side_effects=True, vmem_limit_bytes=56460000
        ),
    )(coefficients, factors)


def solution(mesh):
    placed = (P("src", None, None, "bis"), P("src", None, "bis", None, None))
    return jax.shard_map(
        per_device, mesh=mesh, in_specs=placed, out_specs=P(None, "src", "bis"), check_vma=False
    )
```

time: 132 us -> 26.9 us (0.20)
  waiting for transfers between devices: 81.1 us -> 0 us
  Pallas kernels: 0 us -> 26.1 us
  starting transfers between devices: 14.5 us -> 0 us
  between operations: 13.5 us -> 0.01 us
  local copies, waits for them, and re-layouts: 10.1 us -> 0.62 us
  matrix products: 8.87 us -> 0 us
  other arithmetic: 3.4 us -> 0 us
    psum x1 -> x0, waiting for transfers between devices: 62.8 us -> none  [per_device(): total = lax.psum(flat, 'src')]
    pallas_call x0 -> x1, Pallas kernels: none -> 26.1 us  [per_device(): pl.pallas_call(body, out_shape=jax.ShapeDtypeStruct((2, share, columns),...]
    ppermute x3 -> x0, waiting for transfers between devices: 18.3 us -> none  [swapped(): return lax.ppermute(value, axis, pairs)]
    ppermute x3 -> x0, starting transfers between devices: 14.5 us -> none  [swapped(): return lax.ppermute(value, axis, pairs)]
    dot_general x6 -> x0, matrix products: 8.87 us -> none  [mix_blocks(): jnp.einsum('boj,jbk->obk', factor, stacked, precision=lax.Precision.HIGHEST)]
    another operation x2 -> x0, local copies, waits for them, and re-layouts: 2.58 us -> none  [advance(): return jnp.stack([new_re, new_im], axis=0)]
    slice x3 -> x0, local copies, waits for them, and re-layouts: 2.52 us -> none  [the longest x2 1.59 us: advance(): imag_part = state[1]]
    unnamed x5 -> x1, local copies, waits for them, and re-layouts: 2.6 us -> 0.62 us
  transfers between devices with their start and end apart: 4 -> 0, of which waited for: 4 -> 0; matrix products, arithmetic and copies ran while one was open for 2% -> 0% of each run, Pallas kernels for 0% -> 0%
where the time goes in v2:
time: 26.9 us; the launch traced here: 26.8 us
  Pallas kernels  26.1 us (97%)
  local copies, waits for them, and re-layouts  0.62 us (2%)
    pallas_call x1, Pallas kernels, per_device(): pl.pallas_call(body, out_shape=jax.ShapeDtypeStruct((2, share, columns),...  26.1 us
    unnamed x1, local copies, waits for them, and re-layouts  0.62 us

profile of v2, /device:TPU:1, one launch (start us, length us, event | category | flops | bytes accessed | tf_op | source)
XLA Modules:
  0.0 26.8 jit_solution(9404871252340301275)
XLA Ops:
  0.0 26.1 %shard_map.28 = f32[2,16,256]{2,1,0:T(8,128)S(1)} custom-call(f32[1,2,64,256]{3,2,1,0:T(8,128)} %coef.1, f32[1,3,16,64,256]{4,3,2,1,0:T(8,128)} %fac.1), custom_call_target="tpu_custom_call" | custom-call | tf_op jit(solution)/shard_map/pallas_call | solution.py:204
  26.1 0.6 %copy.4 = f32[2,16,256]{2,1,0:T(8,128)} copy(f32[2,16,256]{2,1,0:T(8,128)S(1)} %shard_map.28) | data formatting | bytes 65536

commit v3 on v2

--- a/solution.py
+++ b/solution.py
@@ -24,8 +24,8 @@
 
 def kernel(steps, groups, rank, blocks, per_block,
            coef, fac, out,
-           start, fbuf, fsplit, first, recv, state, shares,
-           coef_sem, fac_sem, first_sem, send_sem, recv_sem, share_send, share_recv, ready):
+           start, fbuf, fsplit, recv, state, shares,
+           coef_sem, fac_sem, send_sem, recv_sem, share_send, share_recv, ready):
     chunks = blocks * per_block // HALF
     chunk_blocks = blocks // chunks
     rows = chunk_blocks * rank
@@ -41,14 +41,11 @@
                 peer = flipped(peer, 1 << bit)
         peers.append(peer)
 
-    coef_copy = pltpu.make_async_copy(coef.at[0], start, coef_sem)
-    coef_copy.start()
-    fac_copies = [
-        pltpu.make_async_copy(fac.at[0, l], fbuf.at[l], fac_sem.at[l]) for l in range(LEVELS)
-    ]
-    for copy in fac_copies:
-        copy.start()
-
+    coef_copies = []
+    for half in range(chunks // 2):
+        columns = pl.ds(half * LANES, LANES)
+        coef_copies.append(pltpu.make_async_copy(coef.at[0, :, :, columns], start.at[:, :, columns], coef_sem.at[half]))
+        coef_copies[-1].start()
     waits = [bis // steps[1] % 2, bis // steps[2] % 2]
     links = [{"bis": partners[1]}, {"bis": partners[2]}]
     for k in range(1, groups):
@@ -67,20 +64,17 @@
         def _():
             pl.semaphore_wait(ready.at[i], 1)
 
-    first_copy = pltpu.make_async_remote_copy(
-        src_ref=coef.at[0, :, :, pl.ds(0, LANES)],
-        dst_ref=first,
-        send_sem=first_sem.at[0],
-        recv_sem=first_sem.at[1],
-        device_id={"bis": partners[0]},
-        device_id_type=MESH,
-    )
-    first_copy.start()
-
     for i, (late, link) in enumerate(zip(waits, links)):
         @pl.when(late == 1)
         def _(i=i, link=link):
             pl.semaphore_signal(ready.at[i], inc=1, device_id=link, device_id_type=MESH)
+
+    fac_copies = [
+        pltpu.make_async_copy(fac.at[0, l], fbuf.at[l], fac_sem.at[l]) for l in range(LEVELS)
+    ]
+    for copy in fac_copies:
+        copy.start()
+
 
     def exchange(level, chunk):
         return pltpu.make_async_remote_copy(
@@ -113,12 +107,12 @@
             real = pltpu.roll(real, HALF, 1)
         return jnp.where(low_half, real, imag)
 
-    coef_copy.wait()
-    for chunk in list(range(2, chunks)) + [0, 1]:
+    for chunk in range(chunks):
         tile = chunk // 2 * LANES
+        if chunk % 2 == 0:
+            coef_copies[chunk // 2].wait()
         state[0, chunk] = packed((start[0, :, tile:tile + LANES], start[1, :, tile:tile + LANES]), chunk)
-        if chunk >= 2:
-            exchange(0, chunk).start()
+        exchange(0, chunk).start()
 
     for level in range(LEVELS):
         fac_copies[level].wait()
@@ -137,13 +131,8 @@
 
     def step(level, chunk):
         own = state[level, chunk]
-        if level == 0 and chunk < 2:
-            if chunk == 0:
-                first_copy.wait_recv()
-            other = packed((first[0], first[1]), chunk)
-        else:
-            exchange(level, chunk).wait_recv()
-            other = recv[level, chunk]
+        exchange(level, chunk).wait_recv()
+        other = recv[level, chunk]
         weights = jnp.concatenate([own, turned(own, low_half), other, turned(other, low_half)], axis=0)
         high = weights.astype(jnp.bfloat16)
         low = (weights - high.astype(jnp.float32)).astype(jnp.bfloat16)
@@ -182,11 +171,9 @@
         tile = pair * LANES
         out[0, :, tile:tile + LANES] = jnp.where(low_share, totals[0], pltpu.roll(totals[1], HALF, 1))
         out[1, :, tile:tile + LANES] = jnp.where(low_share, pltpu.roll(totals[0], HALF, 1), totals[1])
-    first_copy.wait_send()
     for level in range(LEVELS):
         for chunk in range(chunks):
-            if level > 0 or chunk >= 2:
-                exchange(level, chunk).wait_send()
+            exchange(level, chunk).wait_send()
     for chunk in range(chunks):
         for k in range(groups - 1):
             share_copy(k, chunk).wait_send()
@@ -210,13 +197,11 @@
             pltpu.VMEM((2, rank, columns), jnp.float32),
             pltpu.VMEM((LEVELS, blocks, rank, 4 * rank), jnp.float32),
             pltpu.VMEM((LEVELS, chunks, 2 * blocks // chunks * rank, 4 * rank), jnp.bfloat16),
-            pltpu.VMEM((2, rank, LANES), jnp.float32),
             pltpu.VMEM((LEVELS, chunks, rank, LANES), jnp.float32),
             pltpu.VMEM((LEVELS + 1, chunks, rank, LANES), jnp.float32),
             pltpu.VMEM((groups - 1, chunks, share, LANES), jnp.float32),
-            pltpu.SemaphoreType.DMA,
+            pltpu.SemaphoreType.DMA((chunks // 2,)),
             pltpu.SemaphoreType.DMA((LEVELS,)),
-            pltpu.SemaphoreType.DMA((2,)),
             pltpu.SemaphoreType.DMA((LEVELS, chunks)),
             pltpu.SemaphoreType.DMA((LEVELS, chunks)),
             pltpu.SemaphoreType.DMA((groups - 1, chunks)),

time: 26.9 us -> 26.2 us (0.974)
  Pallas kernels: 26.1 us -> 25.5 us
    pallas_call x1, Pallas kernels: 26.1 us -> 25.5 us  [per_device(): pl.pallas_call(body, out_shape=jax.ShapeDtypeStruct((2, share, columns),...]
where the time goes in v3:
time: 26.2 us; the launch traced here: 26.1 us
  Pallas kernels  25.5 us (97%)
  local copies, waits for them, and re-layouts  0.62 us (2%)
    pallas_call x1, Pallas kernels, per_device(): pl.pallas_call(body, out_shape=jax.ShapeDtypeStruct((2, share, columns),...  25.5 us
    unnamed x1, local copies, waits for them, and re-layouts  0.62 us

profile of v3, /device:TPU:1, one launch (start us, length us, event | category | flops | bytes accessed | tf_op | source)
XLA Modules:
  0.0 26.1 jit_solution(12955813575670560816)
XLA Ops:
  0.0 25.5 %shard_map.28 = f32[2,16,256]{2,1,0:T(8,128)S(1)} custom-call(f32[1,2,64,256]{3,2,1,0:T(8,128)} %coef.1, f32[1,3,16,64,256]{4,3,2,1,0:T(8,128)} %fac.1), custom_call_target="tpu_custom_call" | custom-call | tf_op jit(solution)/shard_map/pallas_call | solution.py:191
  25.5 0.6 %copy.4 = f32[2,16,256]{2,1,0:T(8,128)} copy(f32[2,16,256]{2,1,0:T(8,128)S(1)} %shard_map.28) | data formatting | bytes 65536

commit v4 on v3

--- a/solution.py
+++ b/solution.py
@@ -11,6 +11,7 @@
 MESH = pl.DeviceIdType.MESH
 LANES = 128
 HALF = LANES // 2
+MERGED = (2, 3)
 
 
 def flipped(index, step):
@@ -24,8 +25,8 @@
 
 def kernel(steps, groups, rank, blocks, per_block,
            coef, fac, out,
-           start, fbuf, fsplit, recv, state, shares,
-           coef_sem, fac_sem, send_sem, recv_sem, share_send, share_recv, ready):
+           start, fbuf, fsplit, recv, state, shares, far_factors, fmerged, far_state, far_shares,
+           coef_sem, fac_sem, send_sem, recv_sem, share_send, share_recv, ready, factor_sem, far_send, far_recv):
     chunks = blocks * per_block // HALF
     chunk_blocks = blocks // chunks
     rows = chunk_blocks * rank
@@ -51,6 +52,16 @@
     for k in range(1, groups):
         waits.append(src // 2 % 2 if k >= 2 else 1 - src % 2)
         links.append({"src": peers[k - 1]})
+    for k in range(1, groups):
+        waits.append(bis // steps[2] % 2)
+        links.append({"bis": partners[2], "src": peers[k - 1]})
+    def first_device(link):
+        return jnp.logical_and(link.get("bis", bis) == 0, link.get("src", src) == 0)
+
+    me_first = first_device({})
+    waits = [
+        jnp.where(me_first, 1, jnp.where(first_device(link), 0, late)) for late, link in zip(waits, links)
+    ]
     barrier = pltpu.get_barrier_semaphore()
     pl.semaphore_signal(barrier, inc=1, device_id={"bis": partners[0]}, device_id_type=MESH)
     for late, link in zip(waits, links):
@@ -96,6 +107,32 @@
             device_id_type=MESH,
         )
 
+    far_copies = []
+    for chunk in MERGED:
+        index = (chunk - MERGED[0]) * chunk_blocks
+        far_copies.append(
+            pltpu.make_async_remote_copy(
+                src_ref=fac.at[0, LEVELS - 1, pl.ds(chunk * chunk_blocks, chunk_blocks), :, pl.ds(2 * rank, 2 * rank)],
+                dst_ref=far_factors.at[pl.ds(index, chunk_blocks)],
+                send_sem=factor_sem.at[0, chunk - MERGED[0]],
+                recv_sem=factor_sem.at[1, chunk - MERGED[0]],
+                device_id={"bis": partners[LEVELS - 1]},
+                device_id_type=MESH,
+            )
+        )
+
+    def far_share(k, chunk):
+        peer = peers[k - 1] if k else src
+        link = {"bis": partners[LEVELS - 1], "src": peer} if k else {"bis": partners[LEVELS - 1]}
+        return pltpu.make_async_remote_copy(
+            src_ref=far_state.at[chunk - MERGED[0], pl.ds(pl.multiple_of(peer * share, share), share), :],
+            dst_ref=far_shares.at[k, chunk - MERGED[0]],
+            send_sem=far_send.at[k, chunk - MERGED[0]],
+            recv_sem=far_recv.at[k, chunk - MERGED[0]],
+            device_id=link,
+            device_id_type=MESH,
+        )
+
     low_half = lax.broadcasted_iota(jnp.int32, (rank, LANES), 1) < HALF
     lane_block = lax.broadcasted_iota(jnp.int32, (rank, LANES), 1) % HALF // per_block
 
@@ -113,6 +150,12 @@
             coef_copies[chunk // 2].wait()
         state[0, chunk] = packed((start[0, :, tile:tile + LANES], start[1, :, tile:tile + LANES]), chunk)
         exchange(0, chunk).start()
+
+    @pl.when(waits[1] == 1)
+    def _():
+        for copy in far_copies:
+            copy.start()
+
 
     for level in range(LEVELS):
         fac_copies[level].wait()
@@ -127,7 +170,57 @@
             fsplit[level, chunk, pl.ds(row + rows, rank), :] = low
             return carry
 
-        lax.fori_loop(0, blocks, split_block, 0)
+        if level < LEVELS - 1:
+            lax.fori_loop(0, blocks, split_block, 0)
+        else:
+            lax.fori_loop(0, MERGED[0] * chunk_blocks, split_block, 0)
+
+    def split_merged(block, far):
+        value = far_factors[block] if far else fbuf[LEVELS - 1, MERGED[0] * chunk_blocks + block, :, :2 * rank]
+        high = value.astype(jnp.bfloat16)
+        low = (value - high.astype(jnp.float32)).astype(jnp.bfloat16)
+        chunk = block // chunk_blocks
+        row = pl.multiple_of(block % chunk_blocks * rank, rank) + far * rows
+        fmerged[chunk, pl.ds(row, rank), :] = high
+        fmerged[chunk, pl.ds(row + 2 * rows, rank), :] = low
+
+    def split_near(block, carry):
+        split_merged(block, 0)
+        return carry
+
+    def split_far(block, carry):
+        split_merged(block, 1)
+        return carry
+
+    lax.fori_loop(0, len(MERGED) * chunk_blocks, split_near, 0)
+
+    def merged(chunk, value):
+        index = chunk - MERGED[0]
+        weights = jnp.concatenate([value, turned(value, low_half)], axis=0)
+        high = weights.astype(jnp.bfloat16)
+        low = (weights - high.astype(jnp.float32)).astype(jnp.bfloat16)
+        product = jnp.dot(
+            fmerged[index, :2 * rows], jnp.concatenate([high, low], axis=1), preferred_element_type=jnp.float32
+        )
+        summed = product[:, :LANES] + product[:, LANES:] + jnp.dot(
+            fmerged[index, 2 * rows:], high, preferred_element_type=jnp.float32
+        )
+        for far in (1, 0):
+            picked = summed[far * rows:far * rows + rank]
+            for b in range(1, chunk_blocks):
+                picked = jnp.where(lane_block == b, summed[far * rows + b * rank:far * rows + (b + 1) * rank], picked)
+            if far:
+                far_state[index] = picked
+            else:
+                state[LEVELS, chunk] = picked
+        for k in range(groups):
+            if chunk == MERGED[0] and k:
+                answered(LEVELS - 1 + groups - 1 + k - 1)
+            far_share(k, chunk).start()
+        for k in range(groups - 1):
+            if chunk == MERGED[0]:
+                answered(LEVELS - 1 + k)
+            share_copy(k, chunk).start()
 
     def step(level, chunk):
         own = state[level, chunk]
@@ -143,20 +236,31 @@
         picked = summed[0:rank]
         for b in range(1, chunk_blocks):
             picked = jnp.where(lane_block == b, summed[b * rank:(b + 1) * rank], picked)
+        if level == LEVELS - 2 and chunk in MERGED:
+            merged(chunk, picked)
+            return
         state[level + 1, chunk] = picked
         if level + 1 < LEVELS:
-            if chunk == 0:
-                answered(level)
+            if chunk == 0 and level == 0:
+                answered(0)
             exchange(level + 1, chunk).start()
         else:
             for k in range(groups - 1):
-                if chunk == 0:
-                    answered(LEVELS - 1 + k)
                 share_copy(k, chunk).start()
 
     for level in range(LEVELS):
-        for chunk in range(chunks):
+        for chunk in range(chunks if level < LEVELS - 1 else MERGED[0]):
+            if level == LEVELS - 2 and chunk in MERGED:
+                index = chunk - MERGED[0]
+                far_copies[index].wait_recv()
+                lax.fori_loop(index * chunk_blocks, (index + 1) * chunk_blocks, split_far, 0)
             step(level, chunk)
+            if level == 0 and chunk == 0:
+                @pl.when(waits[1] == 0)
+                def _():
+                    pl.semaphore_wait(ready.at[1], 1)
+                    for copy in far_copies:
+                        copy.start()
 
     own_rows = pl.ds(pl.multiple_of(src * share, share), share)
     low_share = lax.broadcasted_iota(jnp.int32, (share, LANES), 1) < HALF
@@ -167,13 +271,23 @@
             for k in range(groups - 1):
                 share_copy(k, chunk).wait_recv()
                 total = total + shares[k, chunk]
+            if chunk in MERGED:
+                for k in range(groups):
+                    far_share(k, chunk).wait_recv()
+                    total = total + far_shares[k, chunk - MERGED[0]]
             totals.append(total)
         tile = pair * LANES
         out[0, :, tile:tile + LANES] = jnp.where(low_share, totals[0], pltpu.roll(totals[1], HALF, 1))
         out[1, :, tile:tile + LANES] = jnp.where(low_share, pltpu.roll(totals[0], HALF, 1), totals[1])
     for level in range(LEVELS):
         for chunk in range(chunks):
-            exchange(level, chunk).wait_send()
+            if level < LEVELS - 1 or chunk not in MERGED:
+                exchange(level, chunk).wait_send()
+    for copy in far_copies:
+        copy.wait_send()
+    for chunk in MERGED:
+        for k in range(groups):
+            far_share(k, chunk).wait_send()
     for chunk in range(chunks):
         for k in range(groups - 1):
             share_copy(k, chunk).wait_send()
@@ -200,13 +314,20 @@
             pltpu.VMEM((LEVELS, chunks, rank, LANES), jnp.float32),
             pltpu.VMEM((LEVELS + 1, chunks, rank, LANES), jnp.float32),
             pltpu.VMEM((groups - 1, chunks, share, LANES), jnp.float32),
+            pltpu.VMEM((len(MERGED) * blocks // chunks, rank, 2 * rank), jnp.float32),
+            pltpu.VMEM((len(MERGED), 4 * blocks // chunks * rank, 2 * rank), jnp.bfloat16),
+            pltpu.VMEM((len(MERGED), rank, LANES), jnp.float32),
+            pltpu.VMEM((groups, len(MERGED), share, LANES), jnp.float32),
             pltpu.SemaphoreType.DMA((chunks // 2,)),
             pltpu.SemaphoreType.DMA((LEVELS,)),
             pltpu.SemaphoreType.DMA((LEVELS, chunks)),
             pltpu.SemaphoreType.DMA((LEVELS, chunks)),
             pltpu.SemaphoreType.DMA((groups - 1, chunks)),
             pltpu.SemaphoreType.DMA((groups - 1, chunks)),
-            pltpu.SemaphoreType.REGULAR((LEVELS + groups - 2,)),
+            pltpu.SemaphoreType.REGULAR((LEVELS - 1 + 2 * (groups - 1),)),
+            pltpu.SemaphoreType.DMA((2, len(MERGED))),
+            pltpu.SemaphoreType.DMA((groups, len(MERGED))),
+            pltpu.SemaphoreType.DMA((groups, len(MERGED))),
         ],
         compiler_params=pltpu.CompilerParams(
             collective_id=0, has_side_effects=True, vmem_limit_bytes=56460000

time: 26.2 us -> 25.8 us (0.985)
  Pallas kernels: 25.5 us -> 25 us
    pallas_call x1, Pallas kernels: 25.5 us -> 25 us  [per_device(): pl.pallas_call(body, out_shape=jax.ShapeDtypeStruct((2, share, columns),...]
where the time goes in v4:
time: 25.8 us; the launch traced here: 25.7 us
  Pallas kernels  25 us (97%)
  local copies, waits for them, and re-layouts  0.62 us (2%)
    pallas_call x1, Pallas kernels, per_device(): pl.pallas_call(body, out_shape=jax.ShapeDtypeStruct((2, share, columns),...  25 us
    unnamed x1, local copies, waits for them, and re-layouts  0.62 us

profile of v4, /device:TPU:1, one launch (start us, length us, event | category | flops | bytes accessed | tf_op | source)
XLA Modules:
  0.0 25.7 jit_solution(13632767185966547279)
XLA Ops:
  0.0 25.0 %shard_map.28 = f32[2,16,256]{2,1,0:T(8,128)S(1)} custom-call(f32[1,2,64,256]{3,2,1,0:T(8,128)} %coef.1, f32[1,3,16,64,256]{4,3,2,1,0:T(8,128)} %fac.1), custom_call_target="tpu_custom_call" | custom-call | tf_op jit(solution)/shard_map/pallas_call | solution.py:305
  25.0 0.6 %copy.4 = f32[2,16,256]{2,1,0:T(8,128)} copy(f32[2,16,256]{2,1,0:T(8,128)S(1)} %shard_map.28) | data formatting | bytes 65536

commit v5 on v4

--- a/solution.py
+++ b/solution.py
@@ -199,28 +199,28 @@
         weights = jnp.concatenate([value, turned(value, low_half)], axis=0)
         high = weights.astype(jnp.bfloat16)
         low = (weights - high.astype(jnp.float32)).astype(jnp.bfloat16)
-        product = jnp.dot(
-            fmerged[index, :2 * rows], jnp.concatenate([high, low], axis=1), preferred_element_type=jnp.float32
-        )
-        summed = product[:, :LANES] + product[:, LANES:] + jnp.dot(
-            fmerged[index, 2 * rows:], high, preferred_element_type=jnp.float32
-        )
+        stacked = jnp.concatenate([high, low], axis=1)
         for far in (1, 0):
-            picked = summed[far * rows:far * rows + rank]
+            base = far * rows
+            product = jnp.dot(fmerged[index, base:base + rows], stacked, preferred_element_type=jnp.float32)
+            summed = product[:, :LANES] + product[:, LANES:] + jnp.dot(
+                fmerged[index, 2 * rows + base:3 * rows + base], high, preferred_element_type=jnp.float32
+            )
+            picked = summed[:rank]
             for b in range(1, chunk_blocks):
-                picked = jnp.where(lane_block == b, summed[far * rows + b * rank:far * rows + (b + 1) * rank], picked)
+                picked = jnp.where(lane_block == b, summed[b * rank:(b + 1) * rank], picked)
             if far:
                 far_state[index] = picked
+                for k in reversed(range(groups)):
+                    if chunk == MERGED[0] and k:
+                        answered(LEVELS - 1 + groups - 1 + k - 1)
+                    far_share(k, chunk).start()
             else:
                 state[LEVELS, chunk] = picked
-        for k in range(groups):
-            if chunk == MERGED[0] and k:
-                answered(LEVELS - 1 + groups - 1 + k - 1)
-            far_share(k, chunk).start()
-        for k in range(groups - 1):
-            if chunk == MERGED[0]:
-                answered(LEVELS - 1 + k)
-            share_copy(k, chunk).start()
+                for k in range(groups - 1):
+                    if chunk == MERGED[0]:
+                        answered(LEVELS - 1 + k)
+                    share_copy(k, chunk).start()
 
     def step(level, chunk):
         own = state[level, chunk]

time: 25.8 us -> 25.8 us (level)
  no operation moved by 1% of the time
where the time goes in v5:
time: 25.8 us; the launch traced here: 25.7 us
  Pallas kernels  25 us (97%)
  local copies, waits for them, and re-layouts  0.62 us (2%)
    pallas_call x1, Pallas kernels, per_device(): pl.pallas_call(body, out_shape=jax.ShapeDtypeStruct((2, share, columns),...  25 us
    unnamed x1, local copies, waits for them, and re-layouts  0.62 us

profile of v5, /device:TPU:1, one launch (start us, length us, event | category | flops | bytes accessed | tf_op | source)
XLA Modules:
  0.0 25.7 jit_solution(12486376254593565911)
XLA Ops:
  0.0 25.0 %shard_map.28 = f32[2,16,256]{2,1,0:T(8,128)S(1)} custom-call(f32[1,2,64,256]{3,2,1,0:T(8,128)} %coef.1, f32[1,3,16,64,256]{4,3,2,1,0:T(8,128)} %fac.1), custom_call_target="tpu_custom_call" | custom-call | tf_op jit(solution)/shard_map/pallas_call | solution.py:305
  25.0 0.6 %copy.4 = f32[2,16,256]{2,1,0:T(8,128)} copy(f32[2,16,256]{2,1,0:T(8,128)S(1)} %shard_map.28) | data formatting | bytes 65536

commit v6 on v4

--- a/solution.py
+++ b/solution.py
@@ -264,7 +264,7 @@
 
     own_rows = pl.ds(pl.multiple_of(src * share, share), share)
     low_share = lax.broadcasted_iota(jnp.int32, (share, LANES), 1) < HALF
-    for pair in range(chunks // 2):
+    for pair in reversed(range(chunks // 2)):
         totals = []
         for chunk in (2 * pair, 2 * pair + 1):
             total = state[LEVELS, chunk, own_rows, :]

time: 25.8 us -> 25.8 us (level)
  no operation moved by 1% of the time
where the time goes in v6:
time: 25.8 us; the launch traced here: 25.6 us
  Pallas kernels  24.9 us (97%)
  local copies, waits for them, and re-layouts  0.62 us (2%)
    pallas_call x1, Pallas kernels, per_device(): pl.pallas_call(body, out_shape=jax.ShapeDtypeStruct((2, share, columns),...  24.9 us
    unnamed x1, local copies, waits for them, and re-layouts  0.62 us

profile of v6, /device:TPU:1, one launch (start us, length us, event | category | flops | bytes accessed | tf_op | source)
XLA Modules:
  0.0 25.6 jit_solution(5219998616787337367)
XLA Ops:
  0.0 24.9 %shard_map.28 = f32[2,16,256]{2,1,0:T(8,128)S(1)} custom-call(f32[1,2,64,256]{3,2,1,0:T(8,128)} %coef.1, f32[1,3,16,64,256]{4,3,2,1,0:T(8,128)} %fac.1), custom_call_target="tpu_custom_call" | custom-call | tf_op jit(solution)/shard_map/pallas_call | solution.py:305
  24.9 0.6 %copy.4 = f32[2,16,256]{2,1,0:T(8,128)} copy(f32[2,16,256]{2,1,0:T(8,128)S(1)} %shard_map.28) | data formatting | bytes 65536
